TPU v7x, 128 devices: a whole 4x4x4 slice. The times are simulated.
128 devices in a mesh: seq: 16 (over z_hi, y, core), head: 8 (over x, z_lo).
Axes of the slice: x: 4, y: 4, z: 4 (z_hi: 2, z_lo: 2; z = z_hi * 2 + z_lo), core: 2. Of those that a mesh axis runs over, the one named last changes fastest.
Arguments:
- queries: bfloat16 [128, 16384], P(None, 'head')
- cache_keys: bfloat16 [2, 65536, 1024], P(None, 'seq', 'head'), may hold values from -6 to 6
- cache_values: bfloat16 [2, 65536, 1024], P(None, 'seq', 'head'), may hold values from -6 to 6
- tree_keys: bfloat16 [128, 1024], P(None, 'head')
- tree_values: bfloat16 [128, 1024], P(None, 'head'), may hold values from -6 to 6
- ancestors: int32 [2, 64, 64], replicated, may hold values from 0 to 1, as said below
- filled_extents: int32 [2], replicated, may hold values from 1 to 65536, as said below
- out_weight: bfloat16 [16384, 16384], P('head', 'seq'), may hold values from -0.046875 to 0.046875
- residual: bfloat16 [128, 16384], P(None, 'seq'), may hold values from -6 to 6
- norm_gain: bfloat16 [16384], replicated, may hold values from 0.099609375 to 1.8984375
- vocab_weight: bfloat16 [16384, 65536], P(None, ('seq', 'head'))
- candidates: int32 [128], replicated, may hold values from 0 to 65535
- amateur: float32 [128], replicated, may hold values from -12 to -1
Outputs:
- hidden: bfloat16 [128, 16384], P(None, ('seq', 'head'))
- contrast: float32 [128], replicated
Inputs may be any that keep to these rules, and one draw needn't show every extreme that they name: Rows are nodes; node 0 is the root; every node's parent has a smaller index; ancestors[b, i, i] = 1. Positions 0 to filled_extents[b] - 1 of request b are live; some request has length 65536.
All inputs are finite; a program needn't handle non-finite values.
Results may differ from a plain program's by a relative error of at most 0.006.
Values may be sent and summed in bfloat16 or wider, within the bound.
No kernel may reach another device: no remote copies, remote signals or barrier semaphores. Data moves between devices by JAX's collectives and lax.ppermute only.
A program may use at most 192 MiB of HBM per device.

v0:
```python
import jax
import jax.numpy as jnp
from jax import lax
from jax.sharding import PartitionSpec as P

NODES_REQ = 64
D = 16384
HD = 128
NEG_FILL = -1e30
EPSILON = 1e-05


def joined(x, axis, join):
    gathered = jax.tree.map(
        lambda a, kind: lax.all_gather(a.astype(kind), axis),
        x,
        (jnp.bfloat16, jnp.bfloat16, jnp.bfloat16),
    )

    def take(source):
        return jax.tree.map(
            lambda a, own: lax.dynamic_index_in_dim(a, source, 0, False).astype(own.dtype),
            gathered,
            x,
        )

    return lax.fori_loop(
        1, lax.axis_size(axis), lambda source, state: join(state, take(source)), take(0)
    )


def joined_2(part, axis, combine):
    gathered = jax.tree.map(lambda a: lax.all_gather(a, axis), part)

    def take(source):
        return jax.tree.map(lambda a: lax.dynamic_index_in_dim(a, source, 0, False), gathered)

    return lax.fori_loop(
        1, lax.axis_size(axis), lambda source, state: combine(state, take(source)), take(0)
    )


def blend(former, latter):
    highest = jnp.maximum(former[0], latter[0])
    factor_a = jnp.exp(former[0] - highest)
    factor_b = jnp.exp(latter[0] - highest)
    return (
        highest,
        former[1] * factor_a + latter[1] * factor_b,
        former[2] * factor_a[..., None] + latter[2] * factor_b[..., None],
    )


def join_vocab(former, latter):
    highest = jnp.maximum(former[0], latter[0])
    total = former[1] * jnp.exp(former[0] - highest) + latter[1] * jnp.exp(latter[0] - highest)
    return (highest, total, former[2] + latter[2])


def body(
    queries,
    cache_keys,
    cache_values,
    tree_keys,
    tree_values,
    ancestors,
    filled_extents,
    out_weight,
    residual,
    norm_gain,
    vocab_weight,
    candidates,
    amateur,
):
    requests, element_locations, kv_width = cache_keys.shape
    kv_local = kv_width // HD
    heads_local = queries.shape[1] // HD
    group_size = heads_local // kv_local
    score_scale = HD ** (-0.5)
    grouped = queries.reshape(requests, NODES_REQ, kv_local, group_size, HD)
    stored_lookup_entries = cache_keys.reshape(requests, element_locations, kv_local, HD)
    stored_content_entries = cache_values.reshape(requests, element_locations, kv_local, HD)
    insertion_start_index = lax.axis_index("seq") * element_locations
    entry_validity = (insertion_start_index + jnp.arange(element_locations, dtype=jnp.int32))[
        None, :
    ] < filled_extents[:, None]
    joint_visibility_filter = entry_validity[:, None, None, None, :]
    scores = (
        jnp.einsum(
            "bnkgd,bpkd->bkgnp", grouped, stored_lookup_entries, preferred_element_type=jnp.float32
        )
        * score_scale
    )
    scores = jnp.where(joint_visibility_filter, scores, NEG_FILL)
    local_max = scores.max(-1)
    guessed_branch_lookups = tree_keys.reshape(requests, NODES_REQ, kv_local, HD)
    guessed_branch_contents = tree_values.reshape(requests, NODES_REQ, kv_local, HD)
    tree_live = (ancestors > 0)[:, None, None, :, :]
    tree_scores = (
        jnp.einsum(
            "bnkgd,bjkd->bkgnj", grouped, guessed_branch_lookups, preferred_element_type=jnp.float32
        )
        * score_scale
    )
    tree_scores = jnp.where(tree_live, tree_scores, NEG_FILL)
    tree_max = tree_scores.max(-1)
    tree_weights = jnp.where(tree_live, jnp.exp(tree_scores - tree_max[..., None]), 0.0)
    tree_sum = tree_weights.sum(-1)
    tree_summed = jnp.einsum(
        "bkgnj,bjkd->bkgnd",
        tree_weights.astype(jnp.bfloat16),
        guessed_branch_contents,
        preferred_element_type=jnp.float32,
    )
    weights = jnp.where(joint_visibility_filter, jnp.exp(scores - local_max[..., None]), 0.0)
    weight_sum = weights.sum(-1)
    summed = jnp.einsum(
        "bkgnp,bpkd->bkgnd",
        weights.astype(jnp.bfloat16),
        stored_content_entries,
        preferred_element_type=jnp.float32,
    )
    highest, weight_sum, summed = joined((local_max, weight_sum, summed), "seq", blend)
    highest, weight_sum, summed = blend(
        (highest, weight_sum, summed), (tree_max, tree_sum, tree_summed)
    )
    attended = (
        (summed / weight_sum[..., None])
        .transpose(0, 3, 1, 2, 4)
        .reshape(requests * NODES_REQ, heads_local * HD)
        .astype(jnp.bfloat16)
    )
    projected = jnp.dot(attended, out_weight, preferred_element_type=jnp.float32)
    cols_seq = out_weight.shape[1]
    share_width = cols_seq // lax.axis_size("head")
    vocab_local = vocab_weight.shape[1]
    share = lax.psum_scatter(
        projected.astype(jnp.bfloat16), "head", scatter_dimension=1, tiled=True
    ).astype(jnp.float32)
    residual_part = lax.dynamic_slice_in_dim(
        residual, lax.axis_index("head") * share_width, share_width, 1
    )
    hidden = (residual_part.astype(jnp.float32) + share).astype(jnp.bfloat16)
    hidden_f = hidden.astype(jnp.float32)
    squares = lax.psum(jnp.sum(hidden_f * hidden_f, axis=1), ("seq", "head"))
    gain_cols = lax.dynamic_slice_in_dim(
        norm_gain, lax.axis_index(("seq", "head")) * share_width, share_width, 0
    )
    normed = (
        hidden_f * lax.rsqrt(squares / D + EPSILON)[:, None] * gain_cols.astype(jnp.float32)
    ).astype(jnp.bfloat16)
    logits = jnp.dot(
        lax.all_gather(normed, ("seq", "head"), axis=1, tiled=True),
        vocab_weight,
        preferred_element_type=jnp.float32,
    )
    vocab_start = lax.axis_index(("seq", "head")) * vocab_local
    peak_logit = logits.max(axis=1)
    mass_sum = jnp.sum(jnp.exp(logits - peak_logit[:, None]), axis=1)
    matches = jnp.arange(vocab_local, dtype=jnp.int32)[None, :] + vocab_start == candidates[:, None]
    chosen = jnp.sum(jnp.where(matches, logits, 0.0), axis=1)
    peak_logit, mass_sum, chosen = joined_2(
        (peak_logit, mass_sum, chosen), ("seq", "head"), join_vocab
    )
    contrast = chosen - (peak_logit + jnp.log(mass_sum)) - amateur
    return (hidden, contrast)


def solution(mesh):
    in_specs = (
        P(None, "head"),
        P(None, "seq", "head"),
        P(None, "seq", "head"),
        P(None, "head"),
        P(None, "head"),
        P(),
        P(),
        P("head", "seq"),
        P(None, "seq"),
        P(),
        P(None, ("seq", "head")),
        P(),
        P(),
    )
    out_specs = (P(None, ("seq", "head")), P())
    return jax.shard_map(body, mesh=mesh, in_specs=in_specs, out_specs=out_specs, check_vma=False)
```

profile of v0, /device:TPU:0, one launch (start us, length us, event | category | flops | bytes accessed | tf_op | source)
XLA Modules:
  0.0 1467.3 jit_solution(13490291166868993872)
XLA Ops:
  7.2 1.3 copy.49
  8.5 0.7 broadcast_compare_fusion.1
  9.3 13.6 bitcast_reduce_fusion
  22.9 14.7 %fusion.29 = bf16[2,16,64,128]{3,2,1,0:T(8,128)(2,1)} fusion(bf16[2,4096,128]{2,1,0:T(8,128)(2,1)S(1)} %copy-done.7, f32[2,4096,64,16]{1,2,3,0:T(8,128)} %get-tuple-element.428, f32[2,16,64]{2,1,0:T(8,128)S(1)} %get-tuple-element.427, pred[2,4096]{1,0:T(4,128)(4,1)S(1)} %broadcast_compare_fusion.1), kind=kOutput, calls=%fused_computation.41 | convolution fusion | flops 2189688832 | bytes 36192256 | tf_op jit(solution)/shard_map/bkgnp,bpkd->bkgnd/dot_general | solution.py:117
  37.7 0.0 reduce-scatter.4.cloned.1.call-start
  37.8 0.1 copy.37
  37.9 25.8 %all-gather = bf16[32,16,64]{2,1,0:T(8,128)(2,1)S(1)} all-gather(bf16[2,16,64]{2,1,0:T(8,128)(2,1)S(1)} %convert_element_type.176), channel_id=2, replica_groups=mesh['seq'=16,'head'=8] {'seq'}, dimensions={0}, use_global_device_ids=true | all-gather | bytes 69632 | tf_op jit(solution)/shard_map/all_gather | solution.py:15
  63.7 16.1 %fusion.15 = bf16[2,16,64]{2,1,0:T(8,128)(2,1)S(1)} fusion(f32[2,4096,64,16]{1,2,3,0:T(8,128)} %get-tuple-element.428, f32[2,16,64]{2,1,0:T(8,128)S(1)} %get-tuple-element.427, pred[2,4096]{1,0:T(4,128)(4,1)S(1)} %broadcast_compare_fusion.1), kind=kLoop, calls=%fused_computation.26 | loop fusion | flops 41940992 | bytes 33574912 | tf_op jit(solution)/shard_map/reduce_sum | solution.py:116
  79.8 19.8 %all-gather.1 = bf16[32,16,64]{2,1,0:T(8,128)(2,1)S(1)} all-gather(bf16[2,16,64]{2,1,0:T(8,128)(2,1)S(1)} %fusion.15), channel_id=3, replica_groups=mesh['seq'=16,'head'=8] {'seq'}, dimensions={0}, use_global_device_ids=true | all-gather | bytes 69632 | tf_op jit(solution)/shard_map/all_gather | solution.py:15
  99.6 0.6 fusion.64
  100.2 0.2 fusion.36
  100.5 13.1 all-gather.14.cloned.1.call-done
  113.6 1.1 fusion.42
  114.7 31.3 %while.38 = (s32[]{:T(128)}, f32[2,1,16,64]{3,2,1,0:T(8,128)S(1)}, f32[2,1,16,64]{3,2,1,0:T(8,128)S(1)}, f32[2,1,16,64,128]{4,3,2,1,0:T(8,128)S(1)}, bf16[16,2,1...) while((s32[]{:T(128)}, f32[2,1,16,64]{3,2,1,0:T(8,128)S(1)}, ...), condition=%wide.region_3.4_spmd, body=%wide.region_2.3_spmd.sunk | while | flops 1069061 | bytes 2732187 | solution.py:27
  114.8 2.0 fusion.77
  116.9 2.0 fusion.77
  119.0 2.0 fusion.77
  121.1 2.0 fusion.77
  123.2 2.0 fusion.77
  125.3 2.0 fusion.77
  127.3 2.0 fusion.77
  129.4 2.0 fusion.77
  131.5 2.0 fusion.77
  133.6 2.0 fusion.77
  135.7 2.0 fusion.77
  137.8 2.0 fusion.77
  139.9 2.0 fusion.77
  142.0 2.0 fusion.77
  144.0 2.0 fusion.77
  146.1 1.2 fusion.35
  147.3 0.3 copy.41
  147.7 3.0 convolution_convert_fusion
  150.7 0.8 copy.47
  151.6 0.2 all-gather.12.cloned.1.call-start
  151.8 0.8 dynamic-slice_convert_fusion
  152.6 34.4 %reduce-scatter.4.cloned.1.call-done = bf16[128,128]{1,0:T(8,128)(2,1)} async-done(((bf16[1024,128]{1,0:T(8,128)(2,1)}), bf16[128,128]{1,0:T(8,128)(2,1)}) %reduce-scatter.4.cloned.1.call-update) | async-done | bytes 32784
  187.0 0.9 copy.48
  187.9 0.9 fusion.48
  188.8 62.8 %psum.7 = f32[128]{0:T(128)S(1)} all-reduce(f32[128]{0:T(128)S(1)} %get-tuple-element.419), channel_id=1, replica_groups=mesh['seq'=16,'head'=8] {'seq','head'}, use_global_device_ids=true, to_apply=%region_8.9 | all-reduce | flops 128 | bytes 1024 | tf_op jit(solution)/shard_map/psum | solution.py:145
  251.6 0.7 fusion.50
  252.3 255.9 %all-gather.12.cloned.1.call-done = bf16[128,16384]{1,0:T(8,128)(2,1)} async-done(((bf16[128,128]{1,0:T(8,128)(2,1)}), bf16[128,16384]{1,0:T(8,128)(2,1)}) %all-gather.12.cloned.1.call-update) | async-done | bytes 4194320 | tf_op jit(solution)/shard_map/all_gather | solution.py:153
  508.2 9.5 fusion.65
  517.7 313.6 %all-gather.6 = f32[128,1,128]{2,1,0:T(1,128)S(1)} all-gather(f32[1,1,128]{2,1,0:T(1,128)S(1)} %bitcast.225), channel_id=5, replica_groups=mesh['seq'=16,'head'=8] {'seq','head'}, dimensions={0}, use_global_device_ids=true | all-gather | bytes 66048 | tf_op jit(solution)/shard_map/all_gather | solution.py:33
  831.3 0.2 select_reduce_fusion
  831.5 310.2 %all-gather.7 = f32[128,1,128]{2,1,0:T(1,128)S(1)} all-gather(f32[1,1,128]{2,1,0:T(1,128)S(1)} %bitcast.227), channel_id=6, replica_groups=mesh['seq'=16,'head'=8] {'seq','head'}, dimensions={0}, use_global_device_ids=true | all-gather | bytes 66048 | tf_op jit(solution)/shard_map/all_gather | solution.py:33
  1141.8 312.4 %all-gather.8 = f32[128,1,128]{2,1,0:T(1,128)S(1)} all-gather(f32[1,1,128]{2,1,0:T(1,128)S(1)} %bitcast.226), channel_id=7, replica_groups=mesh['seq'=16,'head'=8] {'seq','head'}, dimensions={0}, use_global_device_ids=true | all-gather | bytes 66048 | tf_op jit(solution)/shard_map/all_gather | solution.py:33
  1454.2 6.0 while.39
  1460.2 0.5 subtract_subtract_fusion
  (205 shorter events, 4.4 us)
Async XLA Ops:
  7.2 2.1 copy-start
  7.2 106.4 %all-gather.14.cloned.1.call-start = ((), (), s32[]{:S(2)}) async-start(), calls=%async_computation.2 | async-start | bytes 8912896 | tf_op jit(solution)/shard_map/all_gather | solution.py:15
  9.3 13.6 copy-start.7
  22.9 14.8 %copy-start.3 = (s32[2,64,64]{2,1,0:T(8,128)S(1)}, s32[2,64,64]{2,1,0:T(8,128)}, u32[]{:S(2)}) copy-start(s32[2,64,64]{2,1,0:T(8,128)} %param.22) | copy-start | bytes 98308
  37.7 149.4 %reduce-scatter.4.cloned.1.call-start = ((), (), s32[]{:S(2)}) async-start(), calls=%async_computation.3 | async-start | bytes 294912
  63.7 35.9 %copy-start.4 = (bf16[128,128]{1,0:T(8,128)(2,1)S(1)}, bf16[128,128]{1,0:T(8,128)(2,1)}, u32[]{:S(2)}) copy-start(bf16[128,128]{1,0:T(8,128)(2,1)} %param.20) | copy-start | bytes 98308
  79.8 66.3 %copy-start.8 = (bf16[128,128]{1,0:T(8,128)(2,1)S(1)}, bf16[128,128]{1,0:T(8,128)(2,1)}, u32[]{:S(2)}) copy-start(bf16[128,128]{1,0:T(8,128)(2,1)} %param.21) | copy-start | bytes 98308
  147.6 1313.1 %copy-start.1 = (bf16[2,4096,128]{2,1,0:T(8,128)(2,1)S(1)}, bf16[2,4096,128]{2,1,0:T(8,128)(2,1)}, u32[]{:S(2)}) copy-start(bf16[2,4096,128]{2,1,0:T(8,128)(2,1)} %param.18) | copy-start | bytes 6291460
  147.6 683.7 %copy-start.5 = (s32[128]{0:T(128)S(1)}, s32[128]{0:T(128)}, u32[]{:S(2)}) copy-start(s32[128]{0:T(128)} %param.28) | copy-start | bytes 1540
  147.7 1312.5 %copy-start.6 = (f32[128]{0:T(128)S(1)}, f32[128]{0:T(128)}, u32[]{:S(2)}) copy-start(f32[128]{0:T(128)} %param.29) | copy-start | bytes 1540
  151.6 356.7 %all-gather.12.cloned.1.call-start = ((), (), s32[]{:S(2)}) async-start(), calls=%async_computation.1 | async-start | bytes 4227072 | tf_op jit(solution)/shard_map/all_gather | solution.py:153
  188.8 1272.0 %copy-start.2 = (bf16[128,128]{1,0:T(8,128)(2,1)}, bf16[128,128]{1,0:T(8,128)(2,1)S(1)}, u32[]{:S(2)}) copy-start(bf16[128,128]{1,0:T(8,128)(2,1)S(1)} %get-tuple-element.420) | copy-start | bytes 98308
Sparse Core Ops, SparseCore 0:
  37.8 75.7 all-gather.13
  151.7 35.2 reduce-scatter.3
  252.4 255.7 all-gather.11
where the time goes:
time: 1470 us
  blocking collectives  1040 us (71%)
  waiting for transfers between devices  303 us (21%)
  other arithmetic  55.5 us (4%)
  matrix products  42.7 us (3%)
    all_gather x3, blocking collectives, joined_2(): gathered = jax.tree.map(lambda a: lax.all_gather(a, axis), part)  936 us
    all_gather x1, waiting for transfers between devices, body(): lax.all_gather(normed, ('seq', 'head'), axis=1, tiled=True)  256 us
    psum x1, blocking collectives, body(): squares = lax.psum(jnp.sum(hidden_f * hidden_f, axis=1), ('seq', 'head'))  62.8 us
    all_gather x2, blocking collectives, joined(): lax.all_gather(a.astype(kind), axis)  45.6 us
    unnamed x4, waiting for transfers between devices  34.5 us
    add x15, other arithmetic, blend(): former[2] * factor_a[..., None] + latter[2] * factor_b[..., None]  30 us
  transfers between devices with their start and end apart: 3, of which 3 were waited for; matrix products, arithmetic and copies ran while one was open for 1% of the time, Pallas kernels for 0%

commit v1 on v0

--- a/solution.py
+++ b/solution.py
@@ -142,7 +142,7 @@
     )
     hidden = (residual_part.astype(jnp.float32) + share).astype(jnp.bfloat16)
     hidden_f = hidden.astype(jnp.float32)
-    squares = lax.psum(jnp.sum(hidden_f * hidden_f, axis=1), ("seq", "head"))
+    squares = jnp.sum(lax.all_gather(jnp.sum(hidden_f * hidden_f, axis=1), ("seq", "head")), axis=0)
     gain_cols = lax.dynamic_slice_in_dim(
         norm_gain, lax.axis_index(("seq", "head")) * share_width, share_width, 0
     )

time: 1470 us -> 1710 us (1.16)
  blocking collectives: 1040 us -> 1290 us
    all_gather x0 -> x1, blocking collectives: none -> 310 us  [body(): lax.all_gather(jnp.sum(hidden_f * hidden_f, axis=1), ('seq', 'head'))]
    psum x1 -> x0, blocking collectives: 62.8 us -> none  [body(): squares = lax.psum(jnp.sum(hidden_f * hidden_f, axis=1), ('seq', 'head'))]
where the time goes in v1:
time: 1710 us
  blocking collectives  1290 us (75%)
  waiting for transfers between devices  301 us (18%)
  other arithmetic  55.6 us (3%)
  matrix products  42.7 us (2%)
    all_gather x3, blocking collectives, joined_2(): gathered = jax.tree.map(lambda a: lax.all_gather(a, axis), part)  936 us
    all_gather x1, blocking collectives, body(): lax.all_gather(jnp.sum(hidden_f * hidden_f, axis=1), ('seq', 'head'))  310 us
    all_gather x1, waiting for transfers between devices, body(): lax.all_gather(normed, ('seq', 'head'), axis=1, tiled=True)  254 us
    all_gather x2, blocking collectives, joined(): lax.all_gather(a.astype(kind), axis)  45.6 us
    unnamed x4, waiting for transfers between devices  34.5 us
  transfers between devices with their start and end apart: 3, of which 3 were waited for; matrix products, arithmetic and copies ran while one was open for 1% of the time, Pallas kernels for 0%

profile of v1, /device:TPU:0, one launch (start us, length us, event | category | flops | bytes accessed | tf_op | source)
XLA Modules:
  0.0 1712.8 jit_solution(8684733451749384064)
XLA Ops:
  7.2 1.3 copy.49
  8.5 0.7 broadcast_compare_fusion.1
  9.3 13.6 bitcast_reduce_fusion
  22.9 14.7 fusion.29
  37.8 0.1 copy.37
  37.9 25.8 %all-gather = bf16[32,16,64]{2,1,0:T(8,128)(2,1)S(1)} all-gather(bf16[2,16,64]{2,1,0:T(8,128)(2,1)S(1)} %convert_element_type.176), channel_id=2, replica_groups=mesh['seq'=16,'head'=8] {'seq'}, dimensions={0}, use_global_device_ids=true | all-gather | bytes 69632 | tf_op jit(solution)/shard_map/all_gather | solution.py:15
  63.7 16.1 fusion.15
  79.8 19.8 %all-gather.1 = bf16[32,16,64]{2,1,0:T(8,128)(2,1)S(1)} all-gather(bf16[2,16,64]{2,1,0:T(8,128)(2,1)S(1)} %fusion.15), channel_id=3, replica_groups=mesh['seq'=16,'head'=8] {'seq'}, dimensions={0}, use_global_device_ids=true | all-gather | bytes 69632 | tf_op jit(solution)/shard_map/all_gather | solution.py:15
  99.6 0.6 fusion.64
  100.2 0.2 fusion.36
  100.5 13.1 all-gather.16.cloned.1.call-done
  113.6 1.1 fusion.42
  114.7 31.3 %while.38 = (s32[]{:T(128)}, f32[2,1,16,64]{3,2,1,0:T(8,128)S(1)}, f32[2,1,16,64]{3,2,1,0:T(8,128)S(1)}, f32[2,1,16,64,128]{4,3,2,1,0:T(8,128)S(1)}, bf16[16,2,1...) while((s32[]{:T(128)}, f32[2,1,16,64]{3,2,1,0:T(8,128)S(1)}, ...), condition=%wide.region_3.4_spmd, body=%wide.region_2.3_spmd.sunk | while | flops 1069061 | bytes 2732187 | solution.py:27
  114.8 2.0 fusion.77
  116.9 2.0 fusion.77
  119.0 2.0 fusion.77
  121.1 2.0 fusion.77
  123.2 2.0 fusion.77
  125.3 2.0 fusion.77
  127.3 2.0 fusion.77
  129.4 2.0 fusion.77
  131.5 2.0 fusion.77
  133.6 2.0 fusion.77
  135.7 2.0 fusion.77
  137.8 2.0 fusion.77
  139.9 2.0 fusion.77
  142.0 2.0 fusion.77
  144.0 2.0 fusion.77
  146.1 1.2 fusion.35
  147.3 0.3 copy.41
  147.7 3.0 convolution_convert_fusion
  150.7 0.8 copy.47
  151.6 0.2 all-gather.14.cloned.1.call-start
  151.8 0.8 dynamic-slice_convert_fusion
  152.6 34.4 %reduce-scatter.4.cloned.1.call-done = bf16[128,128]{1,0:T(8,128)(2,1)} async-done(((bf16[1024,128]{1,0:T(8,128)(2,1)}), bf16[128,128]{1,0:T(8,128)(2,1)}) %reduce-scatter.4.cloned.1.call-update) | async-done | bytes 32784
  187.0 0.9 copy.48
  187.9 0.9 fusion.48
  188.8 310.2 %all-gather.7 = f32[128,1,128]{2,1,0:T(1,128)S(1)} all-gather(f32[1,1,128]{2,1,0:T(1,128)S(1)} %bitcast.229), channel_id=5, replica_groups=mesh['seq'=16,'head'=8] {'seq','head'}, dimensions={0}, use_global_device_ids=true | all-gather | bytes 66048 | tf_op jit(solution)/shard_map/all_gather | solution.py:145
  499.0 0.2 reduce_sum.60
  499.2 0.7 fusion.50
  499.9 253.8 %all-gather.14.cloned.1.call-done = bf16[128,16384]{1,0:T(8,128)(2,1)} async-done(((bf16[128,128]{1,0:T(8,128)(2,1)}), bf16[128,16384]{1,0:T(8,128)(2,1)}) %all-gather.14.cloned.1.call-update) | async-done | bytes 4194320 | tf_op jit(solution)/shard_map/all_gather | solution.py:153
  753.7 9.5 fusion.65
  763.2 313.6 %all-gather.8 = f32[128,1,128]{2,1,0:T(1,128)S(1)} all-gather(f32[1,1,128]{2,1,0:T(1,128)S(1)} %bitcast.226), channel_id=6, replica_groups=mesh['seq'=16,'head'=8] {'seq','head'}, dimensions={0}, use_global_device_ids=true | all-gather | bytes 66048 | tf_op jit(solution)/shard_map/all_gather | solution.py:33
  1076.8 0.2 select_reduce_fusion
  1077.0 310.2 %all-gather.9 = f32[128,1,128]{2,1,0:T(1,128)S(1)} all-gather(f32[1,1,128]{2,1,0:T(1,128)S(1)} %bitcast.228), channel_id=7, replica_groups=mesh['seq'=16,'head'=8] {'seq','head'}, dimensions={0}, use_global_device_ids=true | all-gather | bytes 66048 | tf_op jit(solution)/shard_map/all_gather | solution.py:33
  1387.2 312.4 %all-gather.10 = f32[128,1,128]{2,1,0:T(1,128)S(1)} all-gather(f32[1,1,128]{2,1,0:T(1,128)S(1)} %bitcast.227), channel_id=8, replica_groups=mesh['seq'=16,'head'=8] {'seq','head'}, dimensions={0}, use_global_device_ids=true | all-gather | bytes 66048 | tf_op jit(solution)/shard_map/all_gather | solution.py:33
  1699.7 6.1 while.39
  1705.7 0.5 subtract_subtract_fusion
  (206 shorter events, 4.5 us)
Async XLA Ops:
  7.2 2.1 copy-start
  7.2 106.4 %all-gather.16.cloned.1.call-start = ((), (), s32[]{:S(2)}) async-start(), calls=%async_computation.2 | async-start | bytes 8912896 | tf_op jit(solution)/shard_map/all_gather | solution.py:15
  9.3 13.6 copy-start.7
  22.9 14.8 copy-start.3
  37.7 149.4 %reduce-scatter.4.cloned.1.call-start = ((), (), s32[]{:S(2)}) async-start(), calls=%async_computation.3 | async-start | bytes 294912
  63.7 35.9 %copy-start.4 = (bf16[128,128]{1,0:T(8,128)(2,1)S(1)}, bf16[128,128]{1,0:T(8,128)(2,1)}, u32[]{:S(2)}) copy-start(bf16[128,128]{1,0:T(8,128)(2,1)} %param.20) | copy-start | bytes 98308
  79.8 66.3 %copy-start.8 = (bf16[128,128]{1,0:T(8,128)(2,1)S(1)}, bf16[128,128]{1,0:T(8,128)(2,1)}, u32[]{:S(2)}) copy-start(bf16[128,128]{1,0:T(8,128)(2,1)} %param.21) | copy-start | bytes 98308
  147.6 1558.6 %copy-start.1 = (bf16[2,4096,128]{2,1,0:T(8,128)(2,1)S(1)}, bf16[2,4096,128]{2,1,0:T(8,128)(2,1)}, u32[]{:S(2)}) copy-start(bf16[2,4096,128]{2,1,0:T(8,128)(2,1)} %param.18) | copy-start | bytes 6291460
  147.6 929.2 %copy-start.5 = (s32[128]{0:T(128)S(1)}, s32[128]{0:T(128)}, u32[]{:S(2)}) copy-start(s32[128]{0:T(128)} %param.28) | copy-start | bytes 1540
  147.7 1558.1 %copy-start.6 = (f32[128]{0:T(128)S(1)}, f32[128]{0:T(128)}, u32[]{:S(2)}) copy-start(f32[128]{0:T(128)} %param.29) | copy-start | bytes 1540
  151.6 602.1 %all-gather.14.cloned.1.call-start = ((), (), s32[]{:S(2)}) async-start(), calls=%async_computation.1 | async-start | bytes 4227072 | tf_op jit(solution)/shard_map/all_gather | solution.py:153
  188.8 1517.5 %copy-start.2 = (bf16[128,128]{1,0:T(8,128)(2,1)}, bf16[128,128]{1,0:T(8,128)(2,1)S(1)}, u32[]{:S(2)}) copy-start(bf16[128,128]{1,0:T(8,128)(2,1)S(1)} %get-tuple-element.420) | copy-start | bytes 98308
Sparse Core Ops, SparseCore 0:
  37.8 75.7 all-gather.15
  151.7 35.2 reduce-scatter.3
  500.0 253.6 all-gather.13
